TPU v7x, 32 devices: a whole 2x2x4 slice. The times are simulated.
32 devices in a mesh: row: 16 (over z, y, x), col: 2 (over core).
Axes of the slice: x: 2, y: 2, z: 4, core: 2. Of those that a mesh axis runs over, the one named last changes fastest.
Arguments:
- descriptors: bfloat16 [4096, 20480], P('row', 'col')
- block_mask: int32 [32, 160], P('row', 'col'), may hold values 0 or 1
- config_of: int32 [4096], P('row'), may hold values from 0 to 1023, as said below
Outputs:
- gram: float32 [384, 20480], P('row', 'col')
Inputs may be any that keep to these rules, and one draw needn't show every extreme that they name: `config_of`: each source device's 256 environments name every owner index of row equally often, 256 // 16 times.
All inputs are finite; a program needn't handle non-finite values. No bound on the sum of `block_mask` on one device may be relied on, other than what follows from the above.
Results may differ from a plain program's by a relative error of at most 0.0024.
Values may be sent and summed in bfloat16 or wider, within the bound.
A program may use at most 64 MiB of HBM per device.

v0:
```python
import jax
import jax.numpy as jnp
from jax import lax
from jax.sharding import PartitionSpec as P

PW = 384
CONF_DEV = 64


def body(descriptors, block_mask, config_of):
    rows, width = descriptors.shape
    row_blocks, blocks = block_mask.shape
    marks = block_mask.astype(jnp.bfloat16)[:, None, :, None]
    masked = (
        descriptors.reshape(row_blocks, rows // row_blocks, blocks, width // blocks) * marks
    ).reshape(rows, width)
    peers = lax.axis_size("row")
    per_peer = rows // peers
    owner = config_of // CONF_DEV
    order = jnp.argsort(owner, stable=True)
    outgoing = jnp.take(masked, order, axis=0).reshape(peers, per_peer, width)
    labels = jnp.take(config_of, order).reshape(peers, per_peer)
    arrived, arrived_labels = (
        lax.all_to_all(outgoing, "row", split_axis=0, concat_axis=0, tiled=True),
        lax.all_to_all(labels, "row", split_axis=0, concat_axis=0, tiled=True),
    )
    arrived = arrived.reshape(rows, width)
    local = arrived_labels.reshape(rows) - lax.axis_index("row") * CONF_DEV
    member = (local[None, :] == jnp.arange(CONF_DEV, dtype=jnp.int32)[:, None]).astype(jnp.bfloat16)
    counts = jnp.sum(member.astype(jnp.float32), axis=1)
    sums = jnp.dot(member, arrived, preferred_element_type=jnp.float32)
    means = sums / jnp.maximum(counts, 1.0)[:, None]
    centred = (arrived.astype(jnp.float32) - jnp.take(means, local, axis=0)).astype(jnp.bfloat16)
    part = PW // lax.axis_size("col")
    panel = centred[:, :part]
    factor = 1.0 / (rows * peers)
    contract = (((0,), (0,)), ((), ()))
    partial_gram = (
        lax.dot_general(
            lax.all_gather(panel, "col", axis=1, tiled=True),
            centred,
            contract,
            preferred_element_type=jnp.float32,
        )
        * factor
    )
    gram = lax.psum_scatter(partial_gram, "row", scatter_dimension=0, tiled=True)
    return gram


def solution(mesh):
    in_specs = (P("row", "col"), P("row", "col"), P("row"))
    out_specs = P("row", "col")
    return jax.shard_map(body, mesh=mesh, in_specs=in_specs, out_specs=out_specs, check_vma=False)
```

profile of v0, /device:TPU:0, one launch (start us, length us, event | category | flops | bytes accessed | tf_op | source)
XLA Modules:
  0.0 449.9 jit_solution(15943434768808526090)
XLA Ops:
  6.5 0.7 and_select_fusion
  7.2 3.2 sort.17
  10.4 2.0 gather_fusion.1
  12.4 0.7 select_n.54
  13.1 8.3 %all-to-all-start.1 = ((s32[16,1,16]{2,1,0:T(1,128)}), s32[16,1,16]{2,1,0:T(1,128)S(1)}, u32[]{:S(2)}, u32[]{:S(2)}) async-start(s32[16,1,16]{2,1,0:T(1,128)} %select_n.54), calls=%async_computation.1 | async-start | bytes 16384 | tf_op jit(solution)/shard_map/all_to_all | solution.py:25
  21.4 0.7 convert_element_type.15
  22.1 0.1 broadcast_in_dim.34
  22.2 0.0 copy-start
  22.2 0.7 mul.20
  23.0 1.7 copy-done
  24.7 3.5 bitcast_multiply_fusion
  28.2 14.0 %gather_fusion = bf16[256,10240]{1,0:T(8,128)(2,1)} fusion(bf16[256,10240]{1,0:T(8,128)(2,1)} %bitcast_multiply_fusion, s32[1024]{0:T(1024)S(1)} %pad_clamp_fusion.1), kind=kCustom, calls=%fused_computation | custom fusion | bytes 10486784 | tf_op jit(solution)/shard_map/jit(_take)/gather | solution.py:21
  42.2 5.4 %broadcast_select_fusion = bf16[16,16,10240]{2,1,0:T(8,128)(2,1)} fusion(bf16[16,16,10240]{2,1,0:T(8,128)(2,1)} %bitcast.12, pred[16,16]{1,0:T(8,128)(4,1)S(1)} %broadcast_in_dim.34), kind=kLoop, calls=%fused_computation.7 | loop fusion | flops 2621440 | bytes 10486016 | tf_op jit(solution)/shard_map/jit(_take)/select_n | solution.py:21
  47.6 0.0 all-to-all-done.1
  47.6 7.0 %all-to-all-start = ((bf16[16,16,10240]{2,1,0:T(8,128)(2,1)}), bf16[16,16,10240]{2,1,0:T(8,128)(2,1)}, u32[]{:S(2)}, u32[]{:S(2)}) async-start(bf16[16,16,10240]{2,1,0:T(8,128)(2,1)} %broadcast_select_fusion), calls=%async_computation | async-start | bytes 10485760 | tf_op jit(solution)/shard_map/all_to_all | solution.py:24
  54.5 0.2 reduce-scatter.2.cloned.1.call-start
  54.8 0.5 broadcast.91
  55.3 0.7 fusion.2
  56.0 0.1 sub.37
  56.1 0.1 sub.38
  56.2 0.1 convert_reduce_fusion
  56.3 95.9 %all-to-all-done = bf16[16,16,10240]{2,1,0:T(8,128)(2,1)} async-done(((bf16[16,16,10240]{2,1,0:T(8,128)(2,1)}), bf16[16,16,10240]{2,1,0:T(8,128)(2,1)}, u32[]{:S(2)}, u32[]{:S(2)}) %all-to-all-start) | async-done | bytes 5242912 | tf_op jit(solution)/shard_map/all_to_all | solution.py:24
  152.2 3.5 convolution_divide_fusion
  155.7 7.6 %gather_fusion.2 = f32[256,10240]{1,0:T(8,128)} fusion(f32[64,10240]{1,0:T(8,128)S(1)} %convolution_divide_fusion, s32[1024]{0:T(1024)S(1)} %pad_clamp_fusion), kind=kCustom, calls=%fused_computation.2 | custom fusion | bytes 20972544 | tf_op jit(solution)/shard_map/jit(_take)/gather | solution.py:33
  163.3 9.5 %subtract_convert_fusion = bf16[256,10240]{1,0:T(8,128)(2,1)} fusion(f32[256,10240]{1,0:T(8,128)} %gather_fusion.2, pred[256]{0:T(512)(128)(4,1)S(1)} %compare_and_fusion, bf16[16,16,10240]{2,1,0:T(8,128)(2,1)} %all-to-all-done), kind=kLoop, calls=%fused_computation.5 | loop fusion | flops 10485760 | bytes 20971776 | tf_op jit(solution)/shard_map/convert_element_type | solution.py:33
  172.8 0.9 slice.10
  173.7 0.1 copy.5
  173.8 1.9 all_gather.3
  175.7 10.2 %convolution_multiply_fusion = f32[384,10240]{1,0:T(8,128)} fusion(bf16[256,384]{0,1:T(8,128)(2,1)S(1)} %all_gather.3, bf16[256,10240]{1,0:T(8,128)(2,1)} %subtract_convert_fusion), kind=kOutput, calls=%fused_computation.3 | convolution fusion | flops 2017198080 | bytes 21168128 | tf_op jit(solution)/shard_map/dot_general | solution.py:39
  186.0 0.0 reduce-scatter.2.cloned.1.call-update
  186.0 257.1 %reduce-scatter.2.cloned.1.call-done = f32[24,10240]{1,0:T(8,128)} async-done(((f32[384,10240]{1,0:T(8,128)}), f32[24,10240]{1,0:T(8,128)}) %reduce-scatter.2.cloned.1.call-update) | async-done | bytes 983056 | tf_op jit(solution)/shard_map/reduce_scatter | solution.py:47
  (8 shorter events, 0.1 us)
Async XLA Ops:
  13.1 34.5 %all-to-all-start.1 = ((s32[16,1,16]{2,1,0:T(1,128)}), s32[16,1,16]{2,1,0:T(1,128)S(1)}, u32[]{:S(2)}, u32[]{:S(2)}) async-start(s32[16,1,16]{2,1,0:T(1,128)} %select_n.54), calls=%async_computation.1 | async-start | bytes 16384 | tf_op jit(solution)/shard_map/all_to_all | solution.py:25
  22.2 2.5 copy-start
  47.6 104.6 %all-to-all-start = ((bf16[16,16,10240]{2,1,0:T(8,128)(2,1)}), bf16[16,16,10240]{2,1,0:T(8,128)(2,1)}, u32[]{:S(2)}, u32[]{:S(2)}) async-start(bf16[16,16,10240]{2,1,0:T(8,128)(2,1)} %broadcast_select_fusion), calls=%async_computation | async-start | bytes 10485760 | tf_op jit(solution)/shard_map/all_to_all | solution.py:24
  54.5 388.5 %reduce-scatter.2.cloned.1.call-start = ((), (), s32[]{:S(2)}) async-start(), calls=%async_computation.3 | async-start | bytes 16711680 | tf_op jit(solution)/shard_map/reduce_scatter | solution.py:47
Sparse Core Ops, SparseCore 0:
  186.1 256.9 reduce-scatter.1
where the time goes:
time: 450 us
  waiting for transfers between devices  353 us (78%)
  local copies, waits for them, and re-layouts  28.5 us (6%)
  other arithmetic  23.7 us (5%)
  starting transfers between devices  15.5 us (3%)
  matrix products  13.7 us (3%)
  between operations  13.5 us (3%)
    reduce_scatter x1, waiting for transfers between devices, body(): lax.psum_scatter(partial_gram, 'row', scatter_dimension=0, tiled=True)  257 us
    all_to_all x1, waiting for transfers between devices, body(): lax.all_to_all(outgoing, 'row', split_axis=0, concat_axis=0, tiled=True)  95.9 us
    gather x1, local copies, waits for them, and re-layouts, body(): outgoing = jnp.take(masked, order, axis=0).reshape(peers, per_peer, width)  14 us
    dot_general x1, matrix products, body(): lax.dot_general(lax.all_gather(panel, 'col', axis=1, tiled=True), centred...  10.2 us
    convert_element_type x1, other arithmetic, body(): (arrived.astype(jnp.float32) - jnp.take(means, local, axis=0)).astype(jnp...  9.48 us
  transfers between devices with their start and end apart: 3, of which 2 were waited for; matrix products, arithmetic and copies ran while one was open for 6% of the time, Pallas kernels for 0%

commit v1 on v0

v1 whole, which is shorter than its diff:
```python
import functools
import math

import jax
import jax.numpy as jnp
from jax import lax
from jax.experimental import pallas as pl
from jax.experimental.pallas import tpu as pltpu
from jax.sharding import PartitionSpec as P

PW = 384
CONF_DEV = 64
BLOCK = 128
G = 4
SLOT = 16
F32 = jnp.float32
BF16 = jnp.bfloat16


def remote(src, dst, send, recv, **where):
    return pltpu.make_async_remote_copy(
        src_ref=src, dst_ref=dst, send_sem=send, recv_sem=recv,
        device_id=where, device_id_type=pl.DeviceIdType.MESH,
    )


def kernel(cfg, pext, ocol, orow, marks, x, out,
           perm, asend, arec, bsend, brec, piece, hl, mrec, xrec, xmask, part_sum, from_low, from_high, fin,
           a_s, a_r, b_s, b_r, p_s, p_r, c_s, c_r, m_s, m_r, x_s, x_r, lo_s, lo_r, hi_s, hi_r, f_s, f_r, l_s):
    n, ncol, rows, width, part, wide, tiles, tw, factor = cfg
    line = n // G
    per_plane = PW // line
    per_dev = PW // n
    chunk = width // G
    r = lax.axis_index("row")
    c = lax.axis_index("col")
    z = r // G
    q = r % G

    barrier = pltpu.get_barrier_semaphore()

    @pl.loop(1, n)
    def _(k):
        pl.semaphore_signal(barrier, inc=1, device_id={"row": (r + k) % n}, device_id_type=pl.DeviceIdType.MESH)

    @pl.loop(1, ncol)
    def _(k):
        pl.semaphore_signal(barrier, inc=1, device_id={"col": (c + k) % ncol}, device_id_type=pl.DeviceIdType.MESH)

    first = lax.broadcasted_iota(jnp.int32, (rows, rows), 0)
    second = lax.broadcasted_iota(jnp.int32, (rows, rows), 1)
    before = (ocol[...] == orow[...]) & (first < second)
    rank = jnp.sum(jnp.where(before, 1.0, 0.0), axis=0, keepdims=True)
    place = orow[...].astype(F32) * SLOT + rank
    slots = lax.broadcasted_iota(jnp.int32, (n * SLOT, rows), 0).astype(F32)
    perm[...] = jnp.where(slots == place, 1.0, 0.0).astype(BF16)
    asend[...] = jnp.dot(perm[...], pext[...], preferred_element_type=F32).astype(BF16)
    pl.semaphore_wait(barrier, n - 1 + ncol - 1)

    def slot_rows(k):
        return pl.ds(pl.multiple_of(k * SLOT, SLOT), SLOT)

    def to_owner(k):
        peer = (r + k) % n
        return remote(asend.at[slot_rows(peer), :], arec.at[slot_rows(r), :], a_s.at[k], a_r.at[r], row=peer)

    def from_source(k):
        peer = (r + k) % n
        return remote(asend.at[slot_rows(peer), :], arec.at[slot_rows(peer), :], a_s.at[k], a_r.at[peer], row=peer)

    def to_source(k):
        peer = (r + k) % n
        return remote(bsend.at[slot_rows(peer), :], brec.at[slot_rows(r), :], b_s.at[k], b_r.at[r], row=peer)

    def from_owner(k):
        peer = (r + k) % n
        return remote(bsend.at[slot_rows(peer), :], brec.at[slot_rows(peer), :], b_s.at[k], b_r.at[peer], row=peer)

    def x_cols(dest, t):
        return pl.ds(pl.multiple_of(dest * chunk + t * tw, BLOCK), tw)

    def src_rows(s):
        return pl.ds(pl.multiple_of(s * rows, BLOCK), rows)

    def x_send(t, k):
        mate = (q + k) % G
        return remote(x.at[:, x_cols(mate, t)], xrec.at[t, src_rows(q), :], x_s.at[t, k], x_r.at[t, q], row=z * G + mate)

    def x_from(t, k):
        mate = (q + k) % G
        return remote(x.at[:, x_cols(mate, t)], xrec.at[t, src_rows(mate), :], x_s.at[t, k], x_r.at[t, mate], row=z * G + mate)

    def x_own(t):
        return pltpu.make_async_copy(x.at[:, x_cols(q, t)], xrec.at[t, src_rows(q), :], x_s.at[t, 0])

    def m_send(k):
        mate = (q + k) % G
        return remote(marks.at[mate], mrec.at[q], m_s.at[k], m_r.at[q], row=z * G + mate)

    def m_from(k):
        mate = (q + k) % G
        return remote(marks.at[mate], mrec.at[mate], m_s.at[k], m_r.at[mate], row=z * G + mate)

    def hl_slot(col, s):
        return hl.at[:, pl.ds(pl.multiple_of(col * part, 16), part), src_rows(s)]

    def p_send(k):
        mate = (q + k) % G
        return remote(piece, hl_slot(c, q), p_s.at[k], p_r.at[q], row=z * G + mate)

    def p_from(k):
        mate = (q + k) % G
        return remote(piece, hl_slot(c, mate), p_s.at[k], p_r.at[mate], row=z * G + mate)

    def c_own(j):
        peer = (c + j) % ncol
        return remote(piece, hl_slot(c, q), c_s.at[j, 0], c_r.at[c, q], col=peer)

    def c_relay(j, k):
        peer = (c + j) % ncol
        mate = (q + k) % G
        return remote(hl_slot(c, mate), hl_slot(c, mate), c_s.at[j, k], c_r.at[c, mate], col=peer)

    def c_from(j, k):
        peer = (c + j) % ncol
        mate = (q + k) % G
        return remote(piece, hl_slot(peer, mate), c_s.at[j, k], c_r.at[peer, mate], col=peer)

    own_a = pltpu.make_async_copy(asend.at[slot_rows(r), :], arec.at[slot_rows(r), :], l_s.at[0])
    own_a.start()

    @pl.loop(1, n)
    def _(k):
        to_owner(k).start()

    own_m = pltpu.make_async_copy(marks.at[q], mrec.at[q], l_s.at[1])
    own_m.start()
    for k in range(1, G):
        m_send(k).start()

    def start_x(t):
        for k in (2, 1, 3):
            x_send(t, k).start()
        x_own(t).start()

    start_x(0)

    own_a.wait()

    @pl.loop(1, n)
    def _(k):
        from_source(k).wait_recv()

    arrived = arec[...]
    label = arrived[:, part:part + 1].astype(F32)
    ids = lax.broadcasted_iota(jnp.int32, (n * SLOT, BLOCK), 1).astype(F32) + 1.0
    member = jnp.where((label == ids) & (ids <= CONF_DEV), 1.0, 0.0).astype(BF16)
    same = lax.dot_general(member, member, (((1,), (1,)), ((), ())), preferred_element_type=F32)
    counts = jnp.maximum(jnp.sum(same, axis=1, keepdims=True), 1.0)
    same = same.astype(BF16)
    means = jnp.dot(same, arrived, preferred_element_type=F32) / counts
    high = (arrived.astype(F32) - means).astype(BF16)
    low = -(jnp.dot(same, high, preferred_element_type=F32) / counts)
    bsend[:, :wide] = high
    bsend[:, wide:] = low.astype(BF16)

    own_b = pltpu.make_async_copy(bsend.at[slot_rows(r), :], brec.at[slot_rows(r), :], l_s.at[2])
    own_b.start()

    @pl.loop(1, n)
    def _(k):
        to_source(k).start()

    start_x(1)
    own_b.wait()

    @pl.loop(1, n)
    def _(k):
        from_owner(k).wait_recv()

    back = lax.dot_general(brec[...], perm[...], (((0,), (0,)), ((), ())), preferred_element_type=F32).astype(BF16)
    piece[0] = back[:part]
    piece[1] = back[wide:wide + part]
    own_p = pltpu.make_async_copy(piece, hl_slot(c, q), l_s.at[3])
    own_p.start()
    for k in (2, 1, 3):
        p_send(k).start()

    @pl.loop(1, ncol)
    def _(j):
        c_own(j).start()

    for t in range(2, tiles):
        start_x(t)

    for k in (1, 3, 2):
        p_from(k).wait_recv()

        @pl.loop(1, ncol)
        def _(j, k=k):
            c_relay(j, k).start()

    own_p.wait()
    own_m.wait()
    for k in range(1, G):
        m_from(k).wait_recv()

    @pl.loop(1, ncol)
    def _(j):
        for k in range(G):
            c_from(j, k).wait_recv()

    def rows_of(a):
        return pl.ds(pl.multiple_of(a * per_plane, 8), per_plane)

    def up(t, a):
        return remote(part_sum.at[t, rows_of(a), :], from_low.at[t, rows_of(a), :],
                      lo_s.at[t, a], lo_r.at[t, a], row=(r + G) % n)

    def down(t, a):
        return remote(part_sum.at[t, rows_of(a), :], from_high.at[t, rows_of(a), :],
                      hi_s.at[t, a], hi_r.at[t, a], row=(r + n - G) % n)

    def f_send(t, k):
        mate = (q + k) % G
        return remote(fin.at[t, mate], out.at[:, x_cols(q, t)], f_s.at[t, k], f_r.at[t, q], row=z * G + mate)

    def f_from(t, k):
        mate = (q + k) % G
        return remote(fin.at[t, mate], out.at[:, x_cols(mate, t)], f_s.at[t, k], f_r.at[t, mate], row=z * G + mate)

    def f_own(t):
        return pltpu.make_async_copy(fin.at[t, q], out.at[:, x_cols(q, t)], f_s.at[t, 0])

    def multiply(t):
        x_own(t).wait()
        for k in (1, 3, 2):
            x_from(t, k).wait_recv()
        for s in range(G):
            for b in range(rows // BLOCK):
                span = slice(s * rows + b * BLOCK, s * rows + (b + 1) * BLOCK)
                for w in range(tw // BLOCK):
                    cols = slice(w * BLOCK, (w + 1) * BLOCK)
                    keep = jnp.broadcast_to(mrec[s, t, b:b + 1, w:w + 1], (BLOCK, BLOCK)).astype(BF16)
                    xmask[span, cols] = xrec[t, span, cols] * keep
        part_sum[t] = jnp.dot(hl[0], xmask[...], preferred_element_type=F32) + jnp.dot(
            hl[1], xmask[...], preferred_element_type=F32)

    def forward(t):
        def go_up(i, carry):
            a = line - 1 - i

            @pl.when(z > 0)
            def _():
                up(t, a).wait_recv()
                part_sum[t, rows_of(a), :] += from_low[t, rows_of(a), :]

            up(t, a).start()
            return carry

        lax.fori_loop(0, line - 1 - z, go_up, 0)

        def go_down(a, carry):
            @pl.when(z < line - 1)
            def _():
                down(t, a).wait_recv()
                part_sum[t, rows_of(a), :] += from_high[t, rows_of(a), :]

            down(t, a).start()
            return carry

        lax.fori_loop(0, z, go_down, 0)

    def finish(t):
        @pl.when(z > 0)
        def _():
            up(t, z).wait_recv()
            part_sum[t, rows_of(z), :] += from_low[t, rows_of(z), :]

        @pl.when(z < line - 1)
        def _():
            down(t, z).wait_recv()
            part_sum[t, rows_of(z), :] += from_high[t, rows_of(z), :]

        total = part_sum[t, rows_of(z), :] * factor
        for s in range(G):
            fin[t, s] = total[s * per_dev:(s + 1) * per_dev]
        f_own(t).start()
        for k in (2, 1, 3):
            f_send(t, k).start()

    def step(t, carry):
        multiply(t)
        forward(t)

        @pl.when(t > 0)
        def _():
            finish(t - 1)

        return carry

    lax.fori_loop(0, tiles, step, 0)
    finish(tiles - 1)

    @pl.loop(0, tiles)
    def _(t):
        f_own(t).wait()
        for k in range(1, G):
            f_from(t, k).wait_recv()
            f_send(t, k).wait_send()
            x_send(t, k).wait_send()

        def sent_up(a, carry):
            up(t, a).wait_send()
            return carry

        def sent_down(a, carry):
            down(t, a).wait_send()
            return carry

        lax.fori_loop(z + 1, line, sent_up, 0)
        lax.fori_loop(0, z, sent_down, 0)

    for k in range(1, G):
        m_send(k).wait_send()
        p_send(k).wait_send()

    @pl.loop(1, ncol)
    def _(j):
        c_own(j).wait_send()
        for k in range(1, G):
            c_relay(j, k).wait_send()

    @pl.loop(1, n)
    def _(k):
        to_owner(k).wait_send()
        to_source(k).wait_send()


def body(descriptors, block_mask, config_of):
    n, ncol = lax.axis_size("row"), lax.axis_size("col")
    rows, width = descriptors.shape
    row_blocks, blocks = block_mask.shape
    part = PW // ncol
    wide = -(-(part + 1) // 128) * 128
    chunk_blocks = blocks // G
    tiles = 5 if chunk_blocks % 5 == 0 else 1
    per_tile = chunk_blocks // tiles
    tw = per_tile * BLOCK
    line = n // G
    per_dev = PW // n

    panel = descriptors[:, :part]
    panel_marks = jnp.repeat(jnp.repeat(block_mask.astype(BF16), BLOCK, axis=0), BLOCK, axis=1)[:, :part]
    label = (config_of % CONF_DEV + 1).astype(BF16)[:, None]
    pext = jnp.concatenate([panel * panel_marks, label, jnp.zeros((rows, wide - part - 1), BF16)], axis=1)
    owner = config_of // CONF_DEV
    marks = block_mask.astype(F32).reshape(row_blocks, G, tiles, per_tile).transpose(1, 2, 0, 3)
    marks = jnp.pad(marks, ((0, 0), (0, 0), (0, 8 - row_blocks), (0, 128 - per_tile)))

    cfg = (n, ncol, rows, width, part, wide, tiles, tw, 1.0 / (rows * n))
    vm = pltpu.VMEM
    dma = pltpu.SemaphoreType.DMA
    full = pl.BlockSpec(memory_space=pltpu.VMEM)
    return pl.pallas_call(
        functools.partial(kernel, cfg),
        out_shape=jax.ShapeDtypeStruct((per_dev, width), F32),
        in_specs=[full, full, full, full, pl.BlockSpec(memory_space=pl.ANY)],
        out_specs=full,
        scratch_shapes=[
            vm((n * SLOT, rows), BF16),
            vm((n * SLOT, wide), BF16),
            vm((n * SLOT, wide), BF16),
            vm((n * SLOT, 2 * wide), BF16),
            vm((n * SLOT, 2 * wide), BF16),
            vm((2, part, rows), BF16),
            vm((2, PW, G * rows), BF16),
            vm((G, tiles, 8, 128), F32),
            vm((tiles, G * rows, tw), BF16),
            vm((G * rows, tw), BF16),
            vm((tiles, PW, tw), F32),
            vm((tiles, PW, tw), F32),
            vm((tiles, PW, tw), F32),
            vm((tiles, G, per_dev, tw), F32),
            dma((n,)), dma((n,)), dma((n,)), dma((n,)),
            dma((G,)), dma((G,)), dma((ncol, G)), dma((ncol, G)),
            dma((G,)), dma((G,)), dma((tiles, G)), dma((tiles, G)),
            dma((tiles, line)), dma((tiles, line)), dma((tiles, line)), dma((tiles, line)),
            dma((tiles, G)), dma((tiles, G)), dma((4,)),
        ],
        compiler_params=pltpu.CompilerParams(
            collective_id=0, has_side_effects=True, vmem_limit_bytes=56 * 1024 * 1024),
    )(pext, owner[:, None], owner[None, :], marks, descriptors)


def solution(mesh):
    in_specs = (P("row", "col"), P("row", "col"), P("row"))
    out_specs = P("row", "col")
    return jax.shard_map(body, mesh=mesh, in_specs=in_specs, out_specs=out_specs, check_vma=False)
```

time: 450 us -> 147 us (0.33)
  waiting for transfers between devices: 353 us -> 0 us
  Pallas kernels: 0 us -> 135 us
  other arithmetic: 23.7 us -> 2.45 us
  local copies, waits for them, and re-layouts: 28.5 us -> 9.13 us
  starting transfers between devices: 15.5 us -> 0 us
  matrix products: 13.7 us -> 0 us
  between operations: 13.5 us -> 0.09 us
    reduce_scatter x1 -> x0, waiting for transfers between devices: 257 us -> none  [body(): lax.psum_scatter(partial_gram, 'row', scatter_dimension=0, tiled=True)]
    pallas_call x0 -> x1, Pallas kernels: none -> 135 us  [body(): pl.pallas_call(functools.partial(kernel, cfg), out_shape=jax.ShapeDtypeSt...]
    all_to_all x2 -> x0, waiting for transfers between devices: 95.9 us -> none  [the longest x1 95.9 us: body(): lax.all_to_all(outgoing, 'row', split_axis=0, concat_axis=0, tiled=True)]
    gather x3 -> x0, local copies, waits for them, and re-layouts: 23.5 us -> none  [the longest x1 14 us: body(): outgoing = jnp.take(masked, order, axis=0).reshape(peers, per_peer, width)]
    all_to_all x2 -> x0, starting transfers between devices: 15.3 us -> none  [the longest x1 8.34 us: body(): lax.all_to_all(labels, 'row', split_axis=0, concat_axis=0, tiled=True)]
    dot_general x2 -> x0, matrix products: 13.7 us -> none  [the longest x1 10.2 us: body(): lax.dot_general(lax.all_gather(panel, 'col', axis=1, tiled=True), centred...]
    convert_element_type x2 -> x1, other arithmetic: 10.2 us -> 0.76 us  [body(): block_mask.astype(F32).reshape(row_blocks, G, tiles, per_tile)]
    select_n x4 -> x0, other arithmetic: 5.42 us -> none  [the longest x2 5.41 us: body(): outgoing = jnp.take(masked, order, axis=0).reshape(peers, per_peer, width)]
  transfers between devices with their start and end apart: 3 -> 0, of which waited for: 2 -> 0; matrix products, arithmetic and copies ran while one was open for 6% -> 0% of each run, Pallas kernels for 0% -> 0%
where the time goes in v1:
time: 147 us
  Pallas kernels  135 us (92%)
  local copies, waits for them, and re-layouts  9.13 us (6%)
  other arithmetic  2.45 us (2%)
    pallas_call x1, Pallas kernels, body(): pl.pallas_call(functools.partial(kernel, cfg), out_shape=jax.ShapeDtypeSt...  135 us
    broadcast_in_dim x1, local copies, waits for them, and re-layouts, body(): jnp.repeat(jnp.repeat(block_mask.astype(BF16), BLOCK, axis=0), BLOCK, axi...  3.83 us
    unnamed x6, local copies, waits for them, and re-layouts  3.57 us

profile of v1, /device:TPU:0, one launch (start us, length us, event | category | flops | bytes accessed | tf_op | source)
XLA Modules:
  0.0 146.6 jit_solution(10570995426349983424)
XLA Ops:
  0.0 0.8 fusion.2
  0.8 3.8 %broadcast_in_dim.19 = bf16[256,80,128]{2,1,0:T(8,128)(2,1)S(1)} broadcast(bf16[256,80]{1,0:T(8,128)(2,1)S(1)} %bitcast.12), dimensions={0,1} | broadcast | bytes 5283840 | tf_op jit(solution)/shard_map/broadcast_in_dim | solution.py:354
  4.6 0.0 copy-start.1
  4.6 1.4 copy.10
  6.0 0.9 slice_multiply_fusion
  6.9 0.0 copy-done.1
  6.9 0.0 copy-start
  7.0 0.1 broadcast_in_dim.24
  7.1 0.1 pad.7.clone
  7.1 0.7 maximum_maximum_fusion.pext
  7.9 0.8 copy.6.ocol
  8.7 0.1 reshape.11
  8.8 0.6 pad.4.marks
  9.5 0.0 copy-done
  9.5 134.9 %shard_map.37 = f32[24,10240]{1,0:T(8,128)} custom-call(bf16[256,256]{1,0:T(8,128)(2,1)} %maximum_maximum_fusion.pext, s32[256,1]{1,0:T(8,128)} %copy.6.ocol, s32[1,256]{1,0:T(1,128)} %bitcast.15, f32[4,5,8,128]{3,2,1,0:T(8,128)} %pad.4.marks, bf16[256,10240]{1,0:T(8,128)(2,1)} %x.3), custom_call_target="tpu_custom_call" | custom-call | tf_op jit(solution)/shard_map/pallas_call | solution.py:365
  144.4 2.2 %copy.13 = f32[24,10240]{1,0:T(8,128)} copy(f32[24,10240]{1,0:T(8,128)} %shard_map.37) | data formatting | bytes 1966080
  (4 shorter events, 0.0 us)
Async XLA Ops:
  4.6 2.3 %copy-start.1 = (s32[256]{0:T(256)S(1)}, s32[256]{0:T(256)}, u32[]{:S(2)}) copy-start(s32[256]{0:T(256)} %param.5) | copy-start | bytes 3076
  6.9 2.5 %copy-start = (s32[256]{0:T(256)}, s32[256]{0:T(256)S(1)}, u32[]{:S(2)}) copy-start(s32[256]{0:T(256)S(1)} %get-tuple-element.7) | copy-start | bytes 3076

commit v2 on v1

--- a/solution.py
+++ b/solution.py
@@ -13,6 +13,9 @@
 BLOCK = 128
 G = 4
 SLOT = 16
+TILES = 10
+AHEAD = (0, 1)
+HALF = True
 F32 = jnp.float32
 BF16 = jnp.bfloat16
 
@@ -24,19 +27,22 @@
     )
 
 
-def kernel(cfg, pext, ocol, orow, marks, x, out,
-           perm, asend, arec, bsend, brec, piece, hl, mrec, xrec, xmask, part_sum, from_low, from_high, fin,
-           a_s, a_r, b_s, b_r, p_s, p_r, c_s, c_r, m_s, m_r, x_s, x_r, lo_s, lo_r, hi_s, hi_r, f_s, f_r, l_s):
+def kernel(cfg, ccol, crow, marks, x, out,
+           pext, perm, asend, arec, bsend, brec, piece, hl, mrec, xrec, xmask, part_sum, from_low, from_high, fin,
+           a_s, a_r, b_s, b_r, p_s, p_r, c_s, c_r, m_s, m_r, x_s, x_r, lo_s, lo_r, hi_s, hi_r, f_s, f_r, l_s, half_sum, half_low, half_high):
     n, ncol, rows, width, part, wide, tiles, tw, factor = cfg
     line = n // G
     per_plane = PW // line
     per_dev = PW // n
     chunk = width // G
+    chunk_blocks = chunk // BLOCK
     r = lax.axis_index("row")
     c = lax.axis_index("col")
     z = r // G
     q = r % G
 
+    panel_copy = pltpu.make_async_copy(x.at[:, :wide], pext, l_s.at[4])
+    panel_copy.start()
     barrier = pltpu.get_barrier_semaphore()
 
     @pl.loop(1, n)
@@ -49,11 +55,28 @@
 
     first = lax.broadcasted_iota(jnp.int32, (rows, rows), 0)
     second = lax.broadcasted_iota(jnp.int32, (rows, rows), 1)
-    before = (ocol[...] == orow[...]) & (first < second)
+    shift = CONF_DEV.bit_length() - 1
+    owner = crow[...] >> shift
+    before = ((ccol[...] >> shift) == owner) & (first < second)
     rank = jnp.sum(jnp.where(before, 1.0, 0.0), axis=0, keepdims=True)
-    place = orow[...].astype(F32) * SLOT + rank
+    place = owner.astype(F32) * SLOT + rank
     slots = lax.broadcasted_iota(jnp.int32, (n * SLOT, rows), 0).astype(F32)
     perm[...] = jnp.where(slots == place, 1.0, 0.0).astype(BF16)
+    panel_copy.wait()
+    label = ((ccol[...] & (CONF_DEV - 1)) + 1).astype(F32)
+    lane = lax.broadcasted_iota(jnp.int32, (BLOCK, BLOCK), 1)
+    per_tile = tw // BLOCK
+    for b in range(rows // BLOCK):
+        span = slice(b * BLOCK, (b + 1) * BLOCK)
+        for w in range(wide // BLOCK):
+            cols = slice(w * BLOCK, (w + 1) * BLOCK)
+            keep = jnp.zeros((1, 1), F32)
+            if w * BLOCK < part:
+                keep = marks[w // chunk_blocks, w % chunk_blocks // per_tile, b:b + 1, w % per_tile:w % per_tile + 1]
+            block = pext[span, cols].astype(F32) * jnp.broadcast_to(keep, (BLOCK, BLOCK))
+            if (w + 1) * BLOCK > part:
+                block = jnp.where(lane + w * BLOCK < part, block, jnp.broadcast_to(label[span], (BLOCK, BLOCK)))
+            pext[span, cols] = block.astype(BF16)
     asend[...] = jnp.dot(perm[...], pext[...], preferred_element_type=F32).astype(BF16)
     pl.semaphore_wait(barrier, n - 1 + ncol - 1)
 
@@ -143,7 +166,8 @@
             x_send(t, k).start()
         x_own(t).start()
 
-    start_x(0)
+    for t in range(AHEAD[0]):
+        start_x(t)
 
     own_a.wait()
 
@@ -171,7 +195,8 @@
     def _(k):
         to_source(k).start()
 
-    start_x(1)
+    for t in range(AHEAD[0], AHEAD[1]):
+        start_x(t)
     own_b.wait()
 
     @pl.loop(1, n)
@@ -190,7 +215,7 @@
     def _(j):
         c_own(j).start()
 
-    for t in range(2, tiles):
+    for t in range(AHEAD[1], tiles):
         start_x(t)
 
     for k in (1, 3, 2):
@@ -246,42 +271,80 @@
         part_sum[t] = jnp.dot(hl[0], xmask[...], preferred_element_type=F32) + jnp.dot(
             hl[1], xmask[...], preferred_element_type=F32)
 
+    def up_half(t, a):
+        return remote(half_sum.at[t, rows_of(a), :], half_low.at[t, rows_of(a), :],
+                      lo_s.at[t, a], lo_r.at[t, a], row=(r + G) % n)
+
+    def down_half(t, a):
+        return remote(half_sum.at[t, rows_of(a), :], half_high.at[t, rows_of(a), :],
+                      hi_s.at[t, a], hi_r.at[t, a], row=(r + n - G) % n)
+
+    def either(is_half, half, whole):
+        if HALF:
+            pl.when(is_half)(half)
+            pl.when(jnp.logical_not(is_half))(whole)
+        else:
+            whole()
+
+    def add(t, a, landed):
+        part_sum[t, rows_of(a), :] += landed[t, rows_of(a), :].astype(F32)
+
+    def take_up(t, a):
+        def half():
+            up_half(t, a).wait_recv()
+            add(t, a, half_low)
+
+        def whole():
+            up(t, a).wait_recv()
+            add(t, a, from_low)
+
+        @pl.when(z > 0)
+        def _():
+            either(z == 1, half, whole)
+
+    def take_down(t, a):
+        def half():
+            down_half(t, a).wait_recv()
+            add(t, a, half_high)
+
+        def whole():
+            down(t, a).wait_recv()
+            add(t, a, from_high)
+
+        @pl.when(z < line - 1)
+        def _():
+            either(z == line - 2, half, whole)
+
     def forward(t):
+        if HALF:
+            @pl.when((z == 0) | (z == line - 1))
+            def _():
+                half_sum[t] = part_sum[t].astype(BF16)
+
         def go_up(i, carry):
             a = line - 1 - i
-
-            @pl.when(z > 0)
-            def _():
-                up(t, a).wait_recv()
-                part_sum[t, rows_of(a), :] += from_low[t, rows_of(a), :]
-
-            up(t, a).start()
+            take_up(t, a)
+            either(z == 0, lambda: up_half(t, a).start(), lambda: up(t, a).start())
             return carry
 
-        lax.fori_loop(0, line - 1 - z, go_up, 0)
-
         def go_down(a, carry):
-            @pl.when(z < line - 1)
-            def _():
-                down(t, a).wait_recv()
-                part_sum[t, rows_of(a), :] += from_high[t, rows_of(a), :]
-
-            down(t, a).start()
+            take_down(t, a)
+            either(z == line - 1, lambda: down_half(t, a).start(), lambda: down(t, a).start())
             return carry
 
+        @pl.when(z < line // 2)
+        def _():
+            lax.fori_loop(0, line - 1 - z, go_up, 0)
+
         lax.fori_loop(0, z, go_down, 0)
 
+        @pl.when(z >= line // 2)
+        def _():
+            lax.fori_loop(0, line - 1 - z, go_up, 0)
+
     def finish(t):
-        @pl.when(z > 0)
-        def _():
-            up(t, z).wait_recv()
-            part_sum[t, rows_of(z), :] += from_low[t, rows_of(z), :]
-
-        @pl.when(z < line - 1)
-        def _():
-            down(t, z).wait_recv()
-            part_sum[t, rows_of(z), :] += from_high[t, rows_of(z), :]
-
+        take_up(t, z)
+        take_down(t, z)
         total = part_sum[t, rows_of(z), :] * factor
         for s in range(G):
             fin[t, s] = total[s * per_dev:(s + 1) * per_dev]
@@ -311,11 +374,11 @@
             x_send(t, k).wait_send()
 
         def sent_up(a, carry):
-            up(t, a).wait_send()
+            either(z == 0, lambda: up_half(t, a).wait_send(), lambda: up(t, a).wait_send())
             return carry
 
         def sent_down(a, carry):
-            down(t, a).wait_send()
+            either(z == line - 1, lambda: down_half(t, a).wait_send(), lambda: down(t, a).wait_send())
             return carry
 
         lax.fori_loop(z + 1, line, sent_up, 0)
@@ -344,30 +407,27 @@
     part = PW // ncol
     wide = -(-(part + 1) // 128) * 128
     chunk_blocks = blocks // G
-    tiles = 5 if chunk_blocks % 5 == 0 else 1
+    tiles = next(k for k in (TILES, 5, 1) if chunk_blocks % k == 0)
     per_tile = chunk_blocks // tiles
     tw = per_tile * BLOCK
     line = n // G
     per_dev = PW // n
 
-    panel = descriptors[:, :part]
-    panel_marks = jnp.repeat(jnp.repeat(block_mask.astype(BF16), BLOCK, axis=0), BLOCK, axis=1)[:, :part]
-    label = (config_of % CONF_DEV + 1).astype(BF16)[:, None]
-    pext = jnp.concatenate([panel * panel_marks, label, jnp.zeros((rows, wide - part - 1), BF16)], axis=1)
-    owner = config_of // CONF_DEV
     marks = block_mask.astype(F32).reshape(row_blocks, G, tiles, per_tile).transpose(1, 2, 0, 3)
     marks = jnp.pad(marks, ((0, 0), (0, 0), (0, 8 - row_blocks), (0, 128 - per_tile)))
 
     cfg = (n, ncol, rows, width, part, wide, tiles, tw, 1.0 / (rows * n))
     vm = pltpu.VMEM
     dma = pltpu.SemaphoreType.DMA
+    half = vm((tiles, PW, tw) if HALF else (8, 128), BF16)
     full = pl.BlockSpec(memory_space=pltpu.VMEM)
     return pl.pallas_call(
         functools.partial(kernel, cfg),
         out_shape=jax.ShapeDtypeStruct((per_dev, width), F32),
-        in_specs=[full, full, full, full, pl.BlockSpec(memory_space=pl.ANY)],
+        in_specs=[full, full, full, pl.BlockSpec(memory_space=pl.ANY)],
         out_specs=full,
         scratch_shapes=[
+            vm((rows, wide), BF16),
             vm((n * SLOT, rows), BF16),
             vm((n * SLOT, wide), BF16),
             vm((n * SLOT, wide), BF16),
@@ -386,11 +446,12 @@
             dma((G,)), dma((G,)), dma((ncol, G)), dma((ncol, G)),
             dma((G,)), dma((G,)), dma((tiles, G)), dma((tiles, G)),
             dma((tiles, line)), dma((tiles, line)), dma((tiles, line)), dma((tiles, line)),
-            dma((tiles, G)), dma((tiles, G)), dma((4,)),
+            dma((tiles, G)), dma((tiles, G)), dma((5,)),
+            half, half, half,
         ],
         compiler_params=pltpu.CompilerParams(
             collective_id=0, has_side_effects=True, vmem_limit_bytes=56 * 1024 * 1024),
-    )(pext, owner[:, None], owner[None, :], marks, descriptors)
+    )(config_of[:, None], config_of[None, :], marks, descriptors)
 
 
 def solution(mesh):

time: 147 us -> 110 us (0.75)
  Pallas kernels: 135 us -> 104 us
  local copies, waits for them, and re-layouts: 9.13 us -> 4.51 us
  other arithmetic: 2.45 us -> 0.68 us
    pallas_call x1, Pallas kernels: 135 us -> 104 us  [body(): pl.pallas_call(functools.partial(kernel, cfg), out_shape=jax.ShapeDtypeSt...]
    broadcast_in_dim x5 -> x1, local copies, waits for them, and re-layouts: 4.73 us -> 1.47 us  [body(): config_of[:, None]]
    unnamed x6 -> x1, local copies, waits for them, and re-layouts: 3.57 us -> 2.21 us
where the time goes in v2:
time: 110 us; the launch traced here: 109 us
  Pallas kernels  104 us (95%)
  local copies, waits for them, and re-layouts  4.51 us (4%)
    pallas_call x1, Pallas kernels, body(): pl.pallas_call(functools.partial(kernel, cfg), out_shape=jax.ShapeDtypeSt...  104 us
    unnamed x1, local copies, waits for them, and re-layouts  2.21 us

profile of v2, /device:TPU:0, one launch (start us, length us, event | category | flops | bytes accessed | tf_op | source)
XLA Modules:
  0.0 109.5 jit_solution(15769881068492236682)
XLA Ops:
  0.0 0.7 convert_element_type.5
  0.7 0.1 reshape.3
  0.8 0.7 pad.4.marks
  1.5 1.5 %copy.5.ccol = s32[256,1]{1,0:T(8,128)} copy(s32[256,1]{0,1:T(1,128)} %bitcast.6) | data formatting | bytes 2048 | tf_op jit(solution)/shard_map/broadcast_in_dim | solution.py:454
  3.0 104.3 %shard_map.37 = f32[24,10240]{1,0:T(8,128)} custom-call(s32[256,1]{1,0:T(8,128)} %copy.5.ccol, s32[1,256]{1,0:T(1,128)} %bitcast.7, f32[4,10,8,128]{3,2,1,0:T(8,128)} %pad.4.marks, bf16[256,10240]{1,0:T(8,128)(2,1)} %x.3), custom_call_target="tpu_custom_call" | custom-call | tf_op jit(solution)/shard_map/pallas_call | solution.py:424
  107.3 2.2 %copy.9 = f32[24,10240]{1,0:T(8,128)} copy(f32[24,10240]{1,0:T(8,128)} %shard_map.37) | data formatting | bytes 1966080
  (1 shorter events, 0.0 us)
